TPU v7x, 256 devices: a whole 4x4x8 slice. The times are simulated.
256 devices in a mesh: pipe: 8 (over z_lo, y), dp: 32 (over x, z_hi, core).
Axes of the slice: x: 4, y: 4, z: 8 (z_hi: 4, z_lo: 2; z = z_hi * 2 + z_lo), core: 2. Of those that a mesh axis runs over, the one named last changes fastest.
Arguments:
- inputs: bfloat16 [2, 4096, 2048], P(None, 'dp'), may hold values from -6 to 6
- cotangent: bfloat16 [2, 4096, 2048], P(None, 'dp'), may hold values from -0.125 to 0.125
- joined: int32 [2, 16], replicated, may hold values 0 or 1
- w_qkv: bfloat16 [8, 2048, 1536], P('pipe', 'dp'), may hold values from -0.125 to 0.125
- w_out: bfloat16 [8, 1024, 2048], P('pipe', 'dp'), may hold values from -0.1875 to 0.1875
Outputs:
- grad_qkv: float32 [8, 2048, 1536], P('pipe', 'dp')
- grad_out: float32 [8, 1024, 2048], P('pipe', 'dp')
Inputs may be any that keep to these rules, and one draw needn't show every extreme that they name: joined[m, j] is 1 where bin j of micro-batch m holds one molecule covering both of its blocks, 0 where each block holds its own molecule.
All inputs are finite; a program needn't handle non-finite values.
Results may differ from a plain program's by a relative error of at most 0.028.
Values may be sent and summed in bfloat16 or wider, within the bound.
No kernel may reach another device: no remote copies, remote signals or barrier semaphores. Data moves between devices by JAX's collectives and lax.ppermute only.
A program may use at most 192 MiB of HBM per device.

v0:
```python
import math
import jax
import jax.numpy as jnp
from jax import lax
from jax.sharding import PartitionSpec as P

HEADS = 16
HEAD = 64
KVH = 4
norm_eps = 1e-05


def from_partner(block, axis, apart):
    count = lax.axis_size(axis)
    route = []
    for low in range(count):
        high = low | 1 << apart
        if high != low and high < count:
            route += [(low, high), (high, low)]
    return lax.ppermute(block, axis, route)


def from_behind(value, axis, steps):
    count = lax.axis_size(axis)
    leading, last = (max(0, -steps), min(count, count - steps))
    return lax.ppermute(value, axis, [(source, source + steps) for source in range(leading, last)])


def normalize(hidden):
    widened = hidden.astype(jnp.float32)
    inv_rms = lax.rsqrt(jnp.mean(widened * widened, axis=-1, keepdims=True) + norm_eps)
    return (widened * inv_rms).astype(jnp.bfloat16)


def project(hidden, w_qkv):
    normed = normalize(hidden)
    projected = jnp.dot(normed, w_qkv, preferred_element_type=jnp.float32)
    inner_width = HEADS * HEAD
    kv_width = KVH * HEAD
    queries = projected[:, :inner_width].astype(jnp.bfloat16)
    own_kv = jnp.stack(
        [projected[:, inner_width : inner_width + kv_width], projected[:, inner_width + kv_width :]]
    ).astype(jnp.bfloat16)
    return (normed, queries, own_kv)


def attend(queries, key_rows, value_rows, visible):
    row_count = queries.shape[0]
    key_count = key_rows.shape[0]
    grouped = queries.astype(jnp.float32).reshape(row_count, KVH, HEADS // KVH, HEAD)
    key_heads = key_rows.astype(jnp.float32).reshape(key_count, KVH, HEAD)
    value_heads = value_rows.astype(jnp.float32).reshape(key_count, KVH, HEAD)
    scores = jnp.einsum("tkgd,ukd->kgtu", grouped, key_heads) * (1.0 / math.sqrt(HEAD))
    raised = jnp.exp(scores) * visible
    prob_rows = (raised / jnp.sum(raised, axis=-1, keepdims=True)).astype(jnp.bfloat16)
    prob_rows = lax.optimization_barrier(prob_rows)
    context = jnp.einsum("kgtu,ukd->tkgd", prob_rows.astype(jnp.float32), value_heads)
    return context.reshape(row_count, HEADS * HEAD).astype(jnp.bfloat16)


def attend_pair(queries, own_kv, pair_kv, joined_flag):
    row_count = own_kv.shape[1]
    pair_mask = jnp.where(joined_flag > 0, 1.0, 0.0).astype(jnp.float32) * jnp.ones(
        (row_count,), jnp.float32
    )
    visible = jnp.concatenate([jnp.ones((row_count,), jnp.float32), pair_mask])
    key_rows = jnp.concatenate([own_kv[0], pair_kv[0]])
    value_rows = jnp.concatenate([own_kv[1], pair_kv[1]])
    return attend(queries, key_rows, value_rows, visible)


def attention_choice(queries, own_kv, pair_kv, joined_flag):
    return attend_pair(queries, own_kv, pair_kv, joined_flag)


def finish(hidden, context, w_out):
    return (
        hidden.astype(jnp.float32) + jnp.dot(context, w_out, preferred_element_type=jnp.float32)
    ).astype(jnp.bfloat16)


def attention_grads(upstream, queries, own_kv, pair_kv, joined_flag, w_out):
    d_context = jnp.dot(upstream, w_out.T, preferred_element_type=jnp.float32).astype(jnp.bfloat16)

    def forward_part(query_rows, own_rows, pair_rows):
        return attention_choice(query_rows, own_rows, pair_rows, joined_flag)

    unused, pull = jax.vjp(forward_part, queries, own_kv, pair_kv)
    return pull(d_context)


def input_grads(upstream, hidden, d_query, d_own, back_kv, w_qkv):
    combined = (d_own.astype(jnp.float32) + back_kv.astype(jnp.float32)).astype(jnp.bfloat16)
    d_proj = jnp.concatenate([d_query, combined[0], combined[1]], axis=-1)
    d_normed = jnp.dot(d_proj, w_qkv.T, preferred_element_type=jnp.float32)
    widened = hidden.astype(jnp.float32)
    inv_rms = lax.rsqrt(jnp.mean(widened * widened, axis=-1, keepdims=True) + norm_eps)
    cubed = inv_rms * inv_rms * inv_rms
    d_widened = inv_rms * d_normed - widened * cubed * jnp.mean(
        d_normed * widened, axis=-1, keepdims=True
    )
    previous = (upstream.astype(jnp.float32) + d_widened).astype(jnp.bfloat16)
    return (d_proj, previous)


def keep_slot(store, value, slot_index, active):
    current = lax.dynamic_index_in_dim(store, slot_index, 0, keepdims=False)
    return lax.dynamic_update_index_in_dim(store, jnp.where(active, value, current), slot_index, 0)


def on_device(inputs, cotangent, joined, w_qkv, w_out):
    segments = lax.axis_size("pipe")
    segment_index = lax.axis_index("pipe")
    member = lax.axis_index("dp")
    micro_count = inputs.shape[0]
    row_count = inputs.shape[1]
    model_width = inputs.shape[2]
    full_qkv, full_out = (
        lax.all_gather(w_qkv[0], "dp", axis=0, tiled=True),
        lax.all_gather(w_out[0], "dp", axis=0, tiled=True),
    )
    inner_width = full_out.shape[0]
    proj_width = full_qkv.shape[1]
    kv_width = (proj_width - inner_width) // 2
    bin_flags = lax.dynamic_index_in_dim(joined, member // 2, 1, keepdims=False)
    turn_count = micro_count + segments - 1
    blank_rows = jnp.zeros((row_count, model_width), jnp.bfloat16)
    blank_query = jnp.zeros((row_count, inner_width), jnp.bfloat16)
    blank_kv = jnp.zeros((2, row_count, kv_width), jnp.bfloat16)
    blank_proj = jnp.zeros((row_count, proj_width), jnp.bfloat16)
    stores = tuple(
        (
            jnp.zeros((micro_count,) + shaped.shape, jnp.bfloat16)
            for shaped in (blank_rows, blank_rows, blank_query, blank_kv, blank_kv, blank_query)
        )
    )

    def forward_step(turn, incoming, saved):
        position = turn - segment_index
        active = (position >= 0) & (position < micro_count)
        slot_index = jnp.clip(position, 0, micro_count - 1)
        fresh_rows = lax.dynamic_index_in_dim(
            inputs, jnp.clip(turn, 0, micro_count - 1), 0, keepdims=False
        )
        hidden = jnp.where(segment_index == 0, fresh_rows, incoming)
        joined_flag = bin_flags[slot_index]

        def run_project(state):
            return project(state, full_qkv)

        def skip_project(state):
            return (blank_rows, blank_query, blank_kv)

        normed, queries, own_kv = lax.cond(active, run_project, skip_project, hidden)
        pair_kv = from_partner(own_kv, "dp", 0)

        def run_attend(operands):
            context = attention_choice(operands[0], operands[1], operands[2], joined_flag)
            return (context, finish(operands[3], context, full_out))

        def skip_attend(operands):
            return (blank_query, blank_rows)

        context, result = lax.cond(
            active, run_attend, skip_attend, (queries, own_kv, pair_kv, hidden)
        )
        fresh_values = (hidden, normed, queries, own_kv, pair_kv, context)
        saved = tuple(
            (
                keep_slot(store, value, slot_index, active)
                for store, value in zip(saved, fresh_values)
            )
        )
        return (result, saved)

    def forward_turn(turn, carry):
        result, new_stores = forward_step(turn, carry[0], carry[1])
        return (from_behind(result, "pipe", 1), new_stores)

    carry = lax.fori_loop(0, turn_count - 1, forward_turn, (blank_rows, stores))
    unused, stores = forward_step(turn_count - 1, carry[0], carry[1])
    ledger = (jnp.zeros(full_qkv.shape, jnp.float32), jnp.zeros(full_out.shape, jnp.float32))

    def backward_step(turn, incoming, tally):
        position = turn - (segments - 1 - segment_index)
        active = (position >= 0) & (position < micro_count)
        slot_index = jnp.clip(position, 0, micro_count - 1)
        fresh_rows = lax.dynamic_index_in_dim(
            cotangent, jnp.clip(turn, 0, micro_count - 1), 0, keepdims=False
        )
        upstream = jnp.where(segment_index == segments - 1, fresh_rows, incoming)
        hidden, normed, queries, own_kv, pair_kv, context = tuple(
            (lax.dynamic_index_in_dim(store, slot_index, 0, keepdims=False) for store in stores)
        )
        joined_flag = bin_flags[slot_index]

        def run_first(state):
            return attention_grads(state, queries, own_kv, pair_kv, joined_flag, full_out)

        def skip_first(state):
            return (blank_query, blank_kv, blank_kv)

        d_query, d_own, d_pair = lax.cond(active, run_first, skip_first, upstream)
        back_kv = from_partner(d_pair, "dp", 0)

        def run_second(operands):
            return input_grads(operands[0], hidden, operands[1], operands[2], operands[3], full_qkv)

        def skip_second(operands):
            return (blank_proj, blank_rows)

        d_proj, previous = lax.cond(
            active, run_second, skip_second, (upstream, d_query, d_own, back_kv)
        )

        def run_terms(totals):
            qkv_total = totals[0] + jnp.dot(normed.T, d_proj, preferred_element_type=jnp.float32)
            out_total = totals[1] + jnp.dot(context.T, upstream, preferred_element_type=jnp.float32)
            return (qkv_total, out_total)

        def skip_terms(totals):
            return totals

        tally = lax.cond(active, run_terms, skip_terms, tally)
        return (previous, tally)

    def backward_turn(turn, carry):
        previous, new_tally = backward_step(turn, carry[0], carry[1])
        return (from_behind(previous, "pipe", -1), new_tally)

    carry = lax.fori_loop(0, turn_count - 1, backward_turn, (blank_rows, ledger))
    unused, ledger = backward_step(turn_count - 1, carry[0], carry[1])
    grad_qkv, grad_out = (
        lax.psum_scatter(
            ledger[0].astype(jnp.bfloat16), "dp", scatter_dimension=0, tiled=True
        ).astype(jnp.float32),
        lax.psum_scatter(
            ledger[1].astype(jnp.bfloat16), "dp", scatter_dimension=0, tiled=True
        ).astype(jnp.float32),
    )
    return (grad_qkv[None], grad_out[None])


def solution(mesh):
    return jax.shard_map(
        on_device,
        mesh=mesh,
        in_specs=(
            P(None, "dp", None),
            P(None, "dp", None),
            P(),
            P("pipe", "dp", None),
            P("pipe", "dp", None),
        ),
        out_specs=(P("pipe", "dp", None), P("pipe", "dp", None)),
        check_vma=False,
    )
```

profile of v0, /device:TPU:1, one launch (start us, length us, event | category | flops | bytes accessed | tf_op | source)
XLA Modules:
  0.0 1105.0 jit_solution(1348793310206374245)
XLA Ops:
  10.2 65.1 %all-gather.5.cloned.1.call-done = bf16[1,1024,2048]{2,1,0:T(8,128)(2,1)} async-done(((bf16[1,32,2048]{2,1,0:T(8,128)(2,1)}), bf16[1,1024,2048]{2,1,0:T(8,128)(2,1)}) %all-gather.5.cloned.1.call-update) | async-done | bytes 4194320 | tf_op jit(solution)/shard_map/all_gather | solution.py:120
  75.2 69.0 %all-gather.7.cloned.1.call-done = bf16[1,2048,1536]{2,1,0:T(8,128)(2,1)} async-done(((bf16[1,64,1536]{2,1,0:T(8,128)(2,1)}), bf16[1,2048,1536]{2,1,0:T(8,128)(2,1)}) %all-gather.7.cloned.1.call-update) | async-done | bytes 6291472 | tf_op jit(solution)/shard_map/all_gather | solution.py:119
  148.2 266.3 %while.45 = (s32[]{:T(128)}, bf16[128,2048]{1,0:T(8,128)(2,1)S(1)}, bf16[2,128,2048]{2,1,0:T(8,128)(2,1)}, bf16[2,128,2048]{2,1,0:T(8,128)(2,1)}, bf16[2,128,102...) while((s32[]{:T(128)}, bf16[128,2048]{1,0:T(8,128)(2,1)S(1)}, ...), condition=%wide.region_7.8_spmd, body=%wide.region_0.7_spmd.sunk | while | flops 1484519552 | bytes 54158364 | solution.py:180
  175.5 8.6 collective-permute-done.1
  214.8 8.6 collective-permute-done.1
  233.8 17.5 %collective-permute-start.1 = (bf16[128,2048]{1,0:T(8,128)(2,1)S(1)}, bf16[128,2048]{1,0:T(8,128)(2,1)S(1)}, u32[]{:S(2)}, u32[]{:S(2)}) collective-permute-start(bf16[128,2048]{1,0:T(8,128)(2,1)S(1)} %get-tuple-element.1417), channel_id=1, source_target_pairs={{0,32},{32,64},{64,96},{96,128},{128,160},{160,192},{192,224},{1,3... | collective-permute-start | bytes 1572872 | tf_op jit(solution)/shard_map/while/body/eval_jaxpr/ppermute | solution.py:26
  253.1 9.5 collective-permute-done.1
  279.0 9.5 collective-permute-done.1
  299.0 15.3 %collective-permute-start.1 = (bf16[128,2048]{1,0:T(8,128)(2,1)S(1)}, bf16[128,2048]{1,0:T(8,128)(2,1)S(1)}, u32[]{:S(2)}, u32[]{:S(2)}) collective-permute-start(bf16[128,2048]{1,0:T(8,128)(2,1)S(1)} %get-tuple-element.1417), channel_id=1, source_target_pairs={{0,32},{32,64},{64,96},{96,128},{128,160},{160,192},{192,224},{1,3... | collective-permute-start | bytes 1572872 | tf_op jit(solution)/shard_map/while/body/eval_jaxpr/ppermute | solution.py:26
  316.1 9.5 collective-permute-done.1
  342.0 9.5 collective-permute-done.1
  362.0 15.3 %collective-permute-start.1 = (bf16[128,2048]{1,0:T(8,128)(2,1)S(1)}, bf16[128,2048]{1,0:T(8,128)(2,1)S(1)}, u32[]{:S(2)}, u32[]{:S(2)}) collective-permute-start(bf16[128,2048]{1,0:T(8,128)(2,1)S(1)} %get-tuple-element.1417), channel_id=1, source_target_pairs={{0,32},{32,64},{64,96},{96,128},{128,160},{160,192},{192,224},{1,3... | collective-permute-start | bytes 1572872 | tf_op jit(solution)/shard_map/while/body/eval_jaxpr/ppermute | solution.py:26
  379.1 9.5 collective-permute-done.1
  405.0 9.5 collective-permute-done.1
  439.5 403.7 %while.46 = (s32[]{:T(128)}, bf16[128,2048]{1,0:T(8,128)(2,1)}, f32[2048,1536]{1,0:T(8,128)}, f32[1024,2048]{1,0:T(8,128)}, s32[]{:T(128)}, /*index=5*/pred[]{:T...) while((s32[]{:T(128)}, bf16[128,2048]{1,0:T(8,128)(2,1)}, ...), condition=%wide.region_25.26_spmd, body=%wide.region_14.25_spmd.sunk | while | flops 3045198336 | bytes 92394472 | solution.py:231
  446.2 30.4 %collective-permute-done.3 = bf16[128,2048]{1,0:T(8,128)(2,1)} collective-permute-done((bf16[128,2048]{1,0:T(8,128)(2,1)S(1)}, bf16[128,2048]{1,0:T(8,128)(2,1)}, u32[]{:S(2)}, u32[]{:S(2)}) %collective-permute-start.3) | collective-permute-done | bytes 524320 | tf_op jit(solution)/shard_map/while/body/eval_jaxpr/ppermute | solution.py:26
  483.7 17.0 %collective-permute-done.3 = bf16[128,2048]{1,0:T(8,128)(2,1)} collective-permute-done((bf16[128,2048]{1,0:T(8,128)(2,1)S(1)}, bf16[128,2048]{1,0:T(8,128)(2,1)}, u32[]{:S(2)}, u32[]{:S(2)}) %collective-permute-start.3) | collective-permute-done | bytes 524320 | tf_op jit(solution)/shard_map/while/body/eval_jaxpr/ppermute | solution.py:26
  507.9 23.9 %collective-permute-done.3 = bf16[128,2048]{1,0:T(8,128)(2,1)} collective-permute-done((bf16[128,2048]{1,0:T(8,128)(2,1)S(1)}, bf16[128,2048]{1,0:T(8,128)(2,1)}, u32[]{:S(2)}, u32[]{:S(2)}) %collective-permute-start.3) | collective-permute-done | bytes 524320 | tf_op jit(solution)/shard_map/while/body/eval_jaxpr/ppermute | solution.py:26
  539.0 17.0 %collective-permute-done.3 = bf16[128,2048]{1,0:T(8,128)(2,1)} collective-permute-done((bf16[128,2048]{1,0:T(8,128)(2,1)S(1)}, bf16[128,2048]{1,0:T(8,128)(2,1)}, u32[]{:S(2)}, u32[]{:S(2)}) %collective-permute-start.3) | collective-permute-done | bytes 524320 | tf_op jit(solution)/shard_map/while/body/eval_jaxpr/ppermute | solution.py:26
  563.2 23.9 %collective-permute-done.3 = bf16[128,2048]{1,0:T(8,128)(2,1)} collective-permute-done((bf16[128,2048]{1,0:T(8,128)(2,1)S(1)}, bf16[128,2048]{1,0:T(8,128)(2,1)}, u32[]{:S(2)}, u32[]{:S(2)}) %collective-permute-start.3) | collective-permute-done | bytes 524320 | tf_op jit(solution)/shard_map/while/body/eval_jaxpr/ppermute | solution.py:26
  594.3 16.2 %collective-permute-done.3 = bf16[128,2048]{1,0:T(8,128)(2,1)} collective-permute-done((bf16[128,2048]{1,0:T(8,128)(2,1)S(1)}, bf16[128,2048]{1,0:T(8,128)(2,1)}, u32[]{:S(2)}, u32[]{:S(2)}) %collective-permute-start.3) | collective-permute-done | bytes 524320 | tf_op jit(solution)/shard_map/while/body/eval_jaxpr/ppermute | solution.py:26
  617.8 176.7 %collective-permute-done.3 = bf16[128,2048]{1,0:T(8,128)(2,1)} collective-permute-done((bf16[128,2048]{1,0:T(8,128)(2,1)S(1)}, bf16[128,2048]{1,0:T(8,128)(2,1)}, u32[]{:S(2)}, u32[]{:S(2)}) %collective-permute-start.3) | collective-permute-done | bytes 524320 | tf_op jit(solution)/shard_map/while/body/eval_jaxpr/ppermute | solution.py:26
  795.8 15.6 %conditional.22 = (bf16[128,1024]{0,1:T(8,128)(2,1)}, bf16[2,128,256]{1,2,0:T(8,128)(2,1)S(1)}, bf16[2,128,256]{1,2,0:T(8,128)(2,1)}) conditional(s32[]{:T(128)} %convert_element_type.320, () %tuple.239, (bf16[128,2048]{1,0:T(8,128)(2,1)S(1)}, bf16[1024,2048]{1,0:T(8,128)(2,1)}, bf16[2,2,128,256]{2,3,1,0:T(8,128)(2,1)S(1)}, s32[]{:T(128)}, ...), branch_computations={%region_15.15_spmd, %region_16.18_spmd} | conditional | flops 887359488 | bytes 25934138 | solution.py:203
  814.4 8.2 conditional.23
  823.9 19.2 %conditional.24 = ((f32[2048,1536]{1,0:T(8,128)}, f32[1024,2048]{1,0:T(8,128)})) conditional(s32[]{:T(128)} %convert_element_type.320, (f32[2048,1536]{1,0:T(8,128)}, f32[1024,2048]{1,0:T(8,128)}) %tuple.242, (bf16[2,128,2048]{2,1,0:T(8,128)(2,1)}, s32[]{:T(128)}, bf16[128,1536]{1,0:T(8,128)(2,1)S(1)}, f32[2048,1536]{1,0:T(8,128)}, ...), branch_computations={%region_23.23_spmd, %region_24.24_spmd} | conditional | flops 1347420160 | bytes 43648024 | solution.py:224
  823.9 11.2 %convolution_add_fusion.1 = f32[2048,1536]{1,0:T(8,128)} fusion(f32[2048,1536]{1,0:T(8,128)} %get-tuple-element.966, bf16[128,1536]{1,0:T(8,128)(2,1)S(1)} %get-tuple-element.969, bf16[2,128,2048]{2,1,0:T(8,128)(2,1)} %get-tuple-element.967, s32[]{:T(128)} %get-tuple-element.968), kind=kOutput, calls=%fused_computation.121 | convolution fusion | flops 808452096 | bytes 26083840 | tf_op jit(solution)/shard_map/while/body/eval_jaxpr/cond/branch_1_fun/dot_general | solution.py:217
  835.1 8.0 convolution_add_fusion.2
  844.5 16.6 %conditional.12 = (bf16[128,1024]{0,1:T(8,128)(2,1)}, bf16[2,128,256]{1,2,0:T(8,128)(2,1)}, bf16[2,128,256]{1,2,0:T(8,128)(2,1)}) conditional(s32[]{:T(128)} %convert_element_type.228, () %tuple.147, (bf16[128,2048]{1,0:T(8,128)(2,1)S(1)}, bf16[1024,2048]{1,0:T(8,128)(2,1)}, bf16[2,2,128,256]{2,3,1,0:T(8,128)(2,1)S(1)}, s32[]{:T(128)}, ...), branch_computations={%region_26.27_spmd, %region_27.30_spmd} | conditional | flops 887359488 | bytes 25934154 | solution.py:203
  866.2 19.2 %conditional.14 = ((f32[2048,1536]{1,0:T(8,128)}, f32[1024,2048]{1,0:T(8,128)})) conditional(s32[]{:T(128)} %convert_element_type.228, (f32[2048,1536]{1,0:T(8,128)}, f32[1024,2048]{1,0:T(8,128)}) %tuple.145, (bf16[2,128,2048]{2,1,0:T(8,128)(2,1)}, s32[]{:T(128)}, bf16[128,1536]{1,0:T(8,128)(2,1)S(1)}, f32[2048,1536]{1,0:T(8,128)}, ...), branch_computations={%region_32.33_spmd, %region_33.34_spmd} | conditional | flops 1347420160 | bytes 43648024 | solution.py:224
  866.2 11.2 %convolution_add_fusion.3 = f32[2048,1536]{1,0:T(8,128)} fusion(f32[2048,1536]{1,0:T(8,128)} %get-tuple-element.1008, bf16[128,1536]{1,0:T(8,128)(2,1)S(1)} %get-tuple-element.1011, bf16[2,128,2048]{2,1,0:T(8,128)(2,1)} %get-tuple-element.1009, s32[]{:T(128)} %get-tuple-element.1010), kind=kOutput, calls=%fused_computation.172 | convolution fusion | flops 808452096 | bytes 26083840 | tf_op jit(solution)/shard_map/cond/branch_1_fun/dot_general | solution.py:217
  899.5 85.3 %reduce-scatter.5.cloned.1.call-done = bf16[32,2048]{1,0:T(8,128)(2,1)} async-done(((bf16[1024,2048]{1,0:T(8,128)(2,1)}), bf16[32,2048]{1,0:T(8,128)(2,1)}) %reduce-scatter.5.cloned.1.call-update) | async-done | bytes 131088 | tf_op jit(solution)/shard_map/reduce_scatter | solution.py:237
  986.4 110.4 %reduce-scatter.3.cloned.1.call-done = bf16[64,1536]{1,0:T(8,128)(2,1)} async-done(((bf16[2048,1536]{1,0:T(8,128)(2,1)}), bf16[64,1536]{1,0:T(8,128)(2,1)}) %reduce-scatter.3.cloned.1.call-update) | async-done | bytes 196624 | tf_op jit(solution)/shard_map/reduce_scatter | solution.py:234
  (474 shorter events, 356.8 us)
Async XLA Ops:
  7.2 68.1 %all-gather.5.cloned.1.call-start = ((), (), s32[]{:S(2)}) async-start(), calls=%async_computation.4 | async-start | bytes 4325376 | tf_op jit(solution)/shard_map/all_gather | solution.py:120
  7.9 136.3 %all-gather.7.cloned.1.call-start = ((), (), s32[]{:S(2)}) async-start(), calls=%async_computation.5 | async-start | bytes 6488064 | tf_op jit(solution)/shard_map/all_gather | solution.py:119
  8.6 976.1 %reduce-scatter.5.cloned.1.call-start = ((), (), s32[]{:S(2)}) async-start(), calls=%async_computation.3 | async-start | bytes 4325376 | tf_op jit(solution)/shard_map/reduce_scatter | solution.py:237
  158.3 5.3 collective-permute-start
  171.5 12.7 %collective-permute-start.1 = (bf16[128,2048]{1,0:T(8,128)(2,1)S(1)}, bf16[128,2048]{1,0:T(8,128)(2,1)S(1)}, u32[]{:S(2)}, u32[]{:S(2)}) collective-permute-start(bf16[128,2048]{1,0:T(8,128)(2,1)S(1)} %get-tuple-element.1417), channel_id=1, source_target_pairs={{0,32},{32,64},{64,96},{96,128},{128,160},{160,192},{192,224},{1,3... | collective-permute-start | bytes 1572872 | tf_op jit(solution)/shard_map/while/body/eval_jaxpr/ppermute | solution.py:26
  194.3 5.9 collective-permute-start
  207.9 15.4 %collective-permute-start.1 = (bf16[128,2048]{1,0:T(8,128)(2,1)S(1)}, bf16[128,2048]{1,0:T(8,128)(2,1)S(1)}, u32[]{:S(2)}, u32[]{:S(2)}) collective-permute-start(bf16[128,2048]{1,0:T(8,128)(2,1)S(1)} %get-tuple-element.1417), channel_id=1, source_target_pairs={{0,32},{32,64},{64,96},{96,128},{128,160},{160,192},{192,224},{1,3... | collective-permute-start | bytes 1572872 | tf_op jit(solution)/shard_map/while/body/eval_jaxpr/ppermute | solution.py:26
  228.2 4.9 collective-permute-start
  233.8 28.8 %collective-permute-start.1 = (bf16[128,2048]{1,0:T(8,128)(2,1)S(1)}, bf16[128,2048]{1,0:T(8,128)(2,1)S(1)}, u32[]{:S(2)}, u32[]{:S(2)}) collective-permute-start(bf16[128,2048]{1,0:T(8,128)(2,1)S(1)} %get-tuple-element.1417), channel_id=1, source_target_pairs={{0,32},{32,64},{64,96},{96,128},{128,160},{160,192},{192,224},{1,3... | collective-permute-start | bytes 1572872 | tf_op jit(solution)/shard_map/while/body/eval_jaxpr/ppermute | solution.py:26
  267.4 4.9 collective-permute-start
  273.1 15.4 %collective-permute-start.1 = (bf16[128,2048]{1,0:T(8,128)(2,1)S(1)}, bf16[128,2048]{1,0:T(8,128)(2,1)S(1)}, u32[]{:S(2)}, u32[]{:S(2)}) collective-permute-start(bf16[128,2048]{1,0:T(8,128)(2,1)S(1)} %get-tuple-element.1417), channel_id=1, source_target_pairs={{0,32},{32,64},{64,96},{96,128},{128,160},{160,192},{192,224},{1,3... | collective-permute-start | bytes 1572872 | tf_op jit(solution)/shard_map/while/body/eval_jaxpr/ppermute | solution.py:26
  293.4 4.8 collective-permute-start
  299.0 26.6 %collective-permute-start.1 = (bf16[128,2048]{1,0:T(8,128)(2,1)S(1)}, bf16[128,2048]{1,0:T(8,128)(2,1)S(1)}, u32[]{:S(2)}, u32[]{:S(2)}) collective-permute-start(bf16[128,2048]{1,0:T(8,128)(2,1)S(1)} %get-tuple-element.1417), channel_id=1, source_target_pairs={{0,32},{32,64},{64,96},{96,128},{128,160},{160,192},{192,224},{1,3... | collective-permute-start | bytes 1572872 | tf_op jit(solution)/shard_map/while/body/eval_jaxpr/ppermute | solution.py:26
  330.4 4.8 collective-permute-start
  336.1 15.4 %collective-permute-start.1 = (bf16[128,2048]{1,0:T(8,128)(2,1)S(1)}, bf16[128,2048]{1,0:T(8,128)(2,1)S(1)}, u32[]{:S(2)}, u32[]{:S(2)}) collective-permute-start(bf16[128,2048]{1,0:T(8,128)(2,1)S(1)} %get-tuple-element.1417), channel_id=1, source_target_pairs={{0,32},{32,64},{64,96},{96,128},{128,160},{160,192},{192,224},{1,3... | collective-permute-start | bytes 1572872 | tf_op jit(solution)/shard_map/while/body/eval_jaxpr/ppermute | solution.py:26
  356.3 4.8 collective-permute-start
  362.0 26.6 %collective-permute-start.1 = (bf16[128,2048]{1,0:T(8,128)(2,1)S(1)}, bf16[128,2048]{1,0:T(8,128)(2,1)S(1)}, u32[]{:S(2)}, u32[]{:S(2)}) collective-permute-start(bf16[128,2048]{1,0:T(8,128)(2,1)S(1)} %get-tuple-element.1417), channel_id=1, source_target_pairs={{0,32},{32,64},{64,96},{96,128},{128,160},{160,192},{192,224},{1,3... | collective-permute-start | bytes 1572872 | tf_op jit(solution)/shard_map/while/body/eval_jaxpr/ppermute | solution.py:26
  393.4 4.8 collective-permute-start
  399.1 15.4 %collective-permute-start.1 = (bf16[128,2048]{1,0:T(8,128)(2,1)S(1)}, bf16[128,2048]{1,0:T(8,128)(2,1)S(1)}, u32[]{:S(2)}, u32[]{:S(2)}) collective-permute-start(bf16[128,2048]{1,0:T(8,128)(2,1)S(1)} %get-tuple-element.1417), channel_id=1, source_target_pairs={{0,32},{32,64},{64,96},{96,128},{128,160},{160,192},{192,224},{1,3... | collective-permute-start | bytes 1572872 | tf_op jit(solution)/shard_map/while/body/eval_jaxpr/ppermute | solution.py:26
  419.3 7.1 collective-permute-start.4
  444.8 31.7 %collective-permute-start.3 = (bf16[128,2048]{1,0:T(8,128)(2,1)S(1)}, bf16[128,2048]{1,0:T(8,128)(2,1)}, u32[]{:S(2)}, u32[]{:S(2)}) collective-permute-start(bf16[128,2048]{1,0:T(8,128)(2,1)S(1)} %get-tuple-element.1444), channel_id=1, source_target_pairs={{32,0},{64,32},{96,64},{128,96},{160,128},{192,160},{224,192},{33,... | collective-permute-start | bytes 1572872 | tf_op jit(solution)/shard_map/while/body/eval_jaxpr/ppermute | solution.py:26
  482.3 18.3 %collective-permute-start.3 = (bf16[128,2048]{1,0:T(8,128)(2,1)S(1)}, bf16[128,2048]{1,0:T(8,128)(2,1)}, u32[]{:S(2)}, u32[]{:S(2)}) collective-permute-start(bf16[128,2048]{1,0:T(8,128)(2,1)S(1)} %get-tuple-element.1444), channel_id=1, source_target_pairs={{32,0},{64,32},{96,64},{128,96},{160,128},{192,160},{224,192},{33,... | collective-permute-start | bytes 1572872 | tf_op jit(solution)/shard_map/while/body/eval_jaxpr/ppermute | solution.py:26
  506.5 25.3 %collective-permute-start.3 = (bf16[128,2048]{1,0:T(8,128)(2,1)S(1)}, bf16[128,2048]{1,0:T(8,128)(2,1)}, u32[]{:S(2)}, u32[]{:S(2)}) collective-permute-start(bf16[128,2048]{1,0:T(8,128)(2,1)S(1)} %get-tuple-element.1444), channel_id=1, source_target_pairs={{32,0},{64,32},{96,64},{128,96},{160,128},{192,160},{224,192},{33,... | collective-permute-start | bytes 1572872 | tf_op jit(solution)/shard_map/while/body/eval_jaxpr/ppermute | solution.py:26
  535.6 1.9 collective-permute-start.2
  537.6 18.3 %collective-permute-start.3 = (bf16[128,2048]{1,0:T(8,128)(2,1)S(1)}, bf16[128,2048]{1,0:T(8,128)(2,1)}, u32[]{:S(2)}, u32[]{:S(2)}) collective-permute-start(bf16[128,2048]{1,0:T(8,128)(2,1)S(1)} %get-tuple-element.1444), channel_id=1, source_target_pairs={{32,0},{64,32},{96,64},{128,96},{160,128},{192,160},{224,192},{33,... | collective-permute-start | bytes 1572872 | tf_op jit(solution)/shard_map/while/body/eval_jaxpr/ppermute | solution.py:26
  559.8 1.9 collective-permute-start.2
  561.9 25.3 %collective-permute-start.3 = (bf16[128,2048]{1,0:T(8,128)(2,1)S(1)}, bf16[128,2048]{1,0:T(8,128)(2,1)}, u32[]{:S(2)}, u32[]{:S(2)}) collective-permute-start(bf16[128,2048]{1,0:T(8,128)(2,1)S(1)} %get-tuple-element.1444), channel_id=1, source_target_pairs={{32,0},{64,32},{96,64},{128,96},{160,128},{192,160},{224,192},{33,... | collective-permute-start | bytes 1572872 | tf_op jit(solution)/shard_map/while/body/eval_jaxpr/ppermute | solution.py:26
  593.0 17.6 %collective-permute-start.3 = (bf16[128,2048]{1,0:T(8,128)(2,1)S(1)}, bf16[128,2048]{1,0:T(8,128)(2,1)}, u32[]{:S(2)}, u32[]{:S(2)}) collective-permute-start(bf16[128,2048]{1,0:T(8,128)(2,1)S(1)} %get-tuple-element.1444), channel_id=1, source_target_pairs={{32,0},{64,32},{96,64},{128,96},{160,128},{192,160},{224,192},{33,... | collective-permute-start | bytes 1572872 | tf_op jit(solution)/shard_map/while/body/eval_jaxpr/ppermute | solution.py:26
  616.4 178.0 %collective-permute-start.3 = (bf16[128,2048]{1,0:T(8,128)(2,1)S(1)}, bf16[128,2048]{1,0:T(8,128)(2,1)}, u32[]{:S(2)}, u32[]{:S(2)}) collective-permute-start(bf16[128,2048]{1,0:T(8,128)(2,1)S(1)} %get-tuple-element.1444), channel_id=1, source_target_pairs={{32,0},{64,32},{96,64},{128,96},{160,128},{192,160},{224,192},{33,... | collective-permute-start | bytes 1572872 | tf_op jit(solution)/shard_map/while/body/eval_jaxpr/ppermute | solution.py:26
  812.4 2.0 collective-permute-start.2
  822.6 20.6 %collective-permute-start.3 = (bf16[128,2048]{1,0:T(8,128)(2,1)S(1)}, bf16[128,2048]{1,0:T(8,128)(2,1)}, u32[]{:S(2)}, u32[]{:S(2)}) collective-permute-start(bf16[128,2048]{1,0:T(8,128)(2,1)S(1)} %get-tuple-element.1444), channel_id=1, source_target_pairs={{32,0},{64,32},{96,64},{128,96},{160,128},{192,160},{224,192},{33,... | collective-permute-start | bytes 1572872 | tf_op jit(solution)/shard_map/while/body/eval_jaxpr/ppermute | solution.py:26
  891.5 205.3 %reduce-scatter.3.cloned.1.call-start = ((), (), s32[]{:S(2)}) async-start(), calls=%async_computation.2 | async-start | bytes 6488064 | tf_op jit(solution)/shard_map/reduce_scatter | solution.py:234
  (43 other events, 408.3 us)
Sparse Core Ops, SparseCore 0:
  10.6 64.6 all-gather.4
  77.8 66.3 all-gather.6
  891.6 93.1 reduce-scatter.4
  989.2 107.5 reduce-scatter.2
where the time goes:
time: 1110 us; the launch traced here: 1100 us
  waiting for transfers between devices  720 us (65%)
  local copies, waits for them, and re-layouts  104 us (9%)
  other arithmetic  96.1 us (9%)
  starting transfers between devices  91.3 us (8%)
  matrix products  74.2 us (7%)
  between operations  13.9 us (1%)
    ppermute x16, waiting for transfers between devices, from_behind(): lax.ppermute(value, axis, [(source, source + steps) for source in range(l...  380 us
    reduce_scatter x1, waiting for transfers between devices, on_device(): lax.psum_scatter(ledger[0].astype(jnp.bfloat16), 'dp', scatter_dimension=...  110 us
    reduce_scatter x1, waiting for transfers between devices, on_device(): lax.psum_scatter(ledger[1].astype(jnp.bfloat16), 'dp', scatter_dimension=...  85.3 us
    ppermute x16, starting transfers between devices, from_behind(): lax.ppermute(value, axis, [(source, source + steps) for source in range(l...  76.2 us
    all_gather x1, waiting for transfers between devices, on_device(): lax.all_gather(w_qkv[0], 'dp', axis=0, tiled=True)  69 us
    all_gather x1, waiting for transfers between devices, on_device(): lax.all_gather(w_out[0], 'dp', axis=0, tiled=True)  65.1 us
    dynamic_update_slice x53, other arithmetic, keep_slot(): lax.dynamic_update_index_in_dim(store, jnp.where(active, value, current),...  54.4 us
    dynamic_slice x39, local copies, waits for them, and re-layouts, keep_slot(): current = lax.dynamic_index_in_dim(store, slot_index, 0, keepdims=False)  29.3 us
  transfers between devices with their start and end apart: 38, of which 29 were waited for; matrix products, arithmetic and copies ran while one was open for 8% of the time, Pallas kernels for 0%

commit v1 on v0

--- a/solution.py
+++ b/solution.py
@@ -3,6 +3,7 @@
 import jax.numpy as jnp
 from jax import lax
 from jax.sharding import PartitionSpec as P
+from jax.lax import all_to_all, psum
 
 HEADS = 16
 HEAD = 64
@@ -115,8 +116,14 @@
     micro_count = inputs.shape[0]
     row_count = inputs.shape[1]
     model_width = inputs.shape[2]
+    _treat_sites = lambda peer_axis, values: jnp.concatenate(
+        all_to_all(
+            jnp.stack([values for _ in range(psum(1, axis_name=peer_axis))]), peer_axis, 0, 0
+        ),
+        axis=0,
+    )
     full_qkv, full_out = (
-        lax.all_gather(w_qkv[0], "dp", axis=0, tiled=True),
+        _treat_sites("dp", w_qkv[0]),
         lax.all_gather(w_out[0], "dp", axis=0, tiled=True),
     )
     inner_width = full_out.shape[0]

time: 1110 us -> 1150 us (1.036)
  waiting for transfers between devices: 720 us -> 735 us
  starting transfers between devices: 91.3 us -> 104 us
    all_gather x1 -> x0, waiting for transfers between devices: 69 us -> none  [on_device(): lax.all_gather(w_qkv[0], 'dp', axis=0, tiled=True)]
    all_gather x1, waiting for transfers between devices: 65.1 us -> 129 us  [on_device(): lax.all_gather(w_out[0], 'dp', axis=0, tiled=True)]
    all_to_all x0 -> x1, waiting for transfers between devices: none -> 28.5 us  [on_device(): all_to_all(jnp.stack([values for _ in range(psum(1, axis_name=peer_axis))...]
    all_to_all x0 -> x1, starting transfers between devices: none -> 12.8 us  [on_device(): all_to_all(jnp.stack([values for _ in range(psum(1, axis_name=peer_axis))...]
  transfers between devices with their start and end apart: 38 -> 38, of which waited for: 29 -> 29; matrix products, arithmetic and copies ran while one was open for 8% -> 9% of each run, Pallas kernels for 0% -> 0%
where the time goes in v1:
time: 1150 us
  waiting for transfers between devices  735 us (64%)
  local copies, waits for them, and re-layouts  114 us (10%)
  starting transfers between devices  104 us (9%)
  other arithmetic  100 us (9%)
  matrix products  74.1 us (6%)
  between operations  13.9 us (1%)
    ppermute x16, waiting for transfers between devices, from_behind(): lax.ppermute(value, axis, [(source, source + steps) for source in range(l...  370 us
    all_gather x1, waiting for transfers between devices, on_device(): lax.all_gather(w_out[0], 'dp', axis=0, tiled=True)  129 us
    reduce_scatter x1, waiting for transfers between devices, on_device(): lax.psum_scatter(ledger[0].astype(jnp.bfloat16), 'dp', scatter_dimension=...  111 us
    reduce_scatter x1, waiting for transfers between devices, on_device(): lax.psum_scatter(ledger[1].astype(jnp.bfloat16), 'dp', scatter_dimension=...  86.7 us
    ppermute x16, starting transfers between devices, from_behind(): lax.ppermute(value, axis, [(source, source + steps) for source in range(l...  76.1 us
    dynamic_update_slice x53, other arithmetic, keep_slot(): lax.dynamic_update_index_in_dim(store, jnp.where(active, value, current),...  60.5 us
    dynamic_slice x39, local copies, waits for them, and re-layouts, keep_slot(): current = lax.dynamic_index_in_dim(store, slot_index, 0, keepdims=False)  37.5 us
    all_to_all x1, waiting for transfers between devices, on_device(): all_to_all(jnp.stack([values for _ in range(psum(1, axis_name=peer_axis))...  28.5 us
  transfers between devices with their start and end apart: 38, of which 29 were waited for; matrix products, arithmetic and copies ran while one was open for 9% of the time, Pallas kernels for 0%

profile of v1, /device:TPU:1, one launch (start us, length us, event | category | flops | bytes accessed | tf_op | source)
XLA Modules:
  0.0 1146.5 jit_solution(2429352687327257727)
XLA Ops:
  11.5 12.8 %all-to-all-start = ((bf16[32,64,1536]{2,1,0:T(8,128)(2,1)}), bf16[32,64,1536]{2,1,0:T(8,128)(2,1)}, u32[]{:S(2)}, u32[]{:S(2)}) async-start(bf16[32,64,1536]{2,1,0:T(8,128)(2,1)} %stack.27), calls=%async_computation | async-start | bytes 12582912 | tf_op jit(solution)/shard_map/all_to_all | solution.py:120
  25.8 129.4 %all-gather.3.cloned.1.call-done = bf16[1,1024,2048]{2,1,0:T(8,128)(2,1)} async-done(((bf16[1,32,2048]{2,1,0:T(8,128)(2,1)}), bf16[1,1024,2048]{2,1,0:T(8,128)(2,1)}) %all-gather.3.cloned.1.call-update) | async-done | bytes 4194320 | tf_op jit(solution)/shard_map/all_gather | solution.py:127
  155.2 28.5 %all-to-all-done = bf16[32,64,1536]{2,1,0:T(8,128)(2,1)} async-done(((bf16[32,64,1536]{2,1,0:T(8,128)(2,1)}), bf16[32,64,1536]{2,1,0:T(8,128)(2,1)}, u32[]{:S(2)}, u32[]{:S(2)}) %all-to-all-start) | async-done | bytes 6291488 | tf_op jit(solution)/shard_map/all_to_all | solution.py:120
  188.4 273.9 %while.45 = (s32[]{:T(128)}, bf16[128,2048]{1,0:T(8,128)(2,1)S(1)}, bf16[2,128,2048]{2,1,0:T(8,128)(2,1)}, bf16[2,128,2048]{2,1,0:T(8,128)(2,1)}, bf16[2,128,102...) while((s32[]{:T(128)}, bf16[128,2048]{1,0:T(8,128)(2,1)S(1)}, ...), condition=%wide.region_7.8_spmd, body=%wide.region_0.7_spmd.sunk | while | flops 1484519552 | bytes 54158872 | solution.py:187
  217.4 8.0 collective-permute-done.1
  277.0 17.4 %collective-permute-start.1 = (bf16[128,2048]{1,0:T(8,128)(2,1)S(1)}, bf16[128,2048]{1,0:T(8,128)(2,1)S(1)}, u32[]{:S(2)}, u32[]{:S(2)}) collective-permute-start(bf16[128,2048]{1,0:T(8,128)(2,1)S(1)} %get-tuple-element.1417), channel_id=1, source_target_pairs={{0,32},{32,64},{64,96},{96,128},{128,160},{160,192},{192,224},{1,3... | collective-permute-start | bytes 1572872 | tf_op jit(solution)/shard_map/while/body/eval_jaxpr/ppermute | solution.py:27
  296.8 8.9 collective-permute-done.1
  323.7 8.9 collective-permute-done.1
  344.1 15.2 %collective-permute-start.1 = (bf16[128,2048]{1,0:T(8,128)(2,1)S(1)}, bf16[128,2048]{1,0:T(8,128)(2,1)S(1)}, u32[]{:S(2)}, u32[]{:S(2)}) collective-permute-start(bf16[128,2048]{1,0:T(8,128)(2,1)S(1)} %get-tuple-element.1417), channel_id=1, source_target_pairs={{0,32},{32,64},{64,96},{96,128},{128,160},{160,192},{192,224},{1,3... | collective-permute-start | bytes 1572872 | tf_op jit(solution)/shard_map/while/body/eval_jaxpr/ppermute | solution.py:27
  361.7 8.9 collective-permute-done.1
  388.6 8.9 collective-permute-done.1
  408.9 15.2 %collective-permute-start.1 = (bf16[128,2048]{1,0:T(8,128)(2,1)S(1)}, bf16[128,2048]{1,0:T(8,128)(2,1)S(1)}, u32[]{:S(2)}, u32[]{:S(2)}) collective-permute-start(bf16[128,2048]{1,0:T(8,128)(2,1)S(1)} %get-tuple-element.1417), channel_id=1, source_target_pairs={{0,32},{32,64},{64,96},{96,128},{128,160},{160,192},{192,224},{1,3... | collective-permute-start | bytes 1572872 | tf_op jit(solution)/shard_map/while/body/eval_jaxpr/ppermute | solution.py:27
  426.6 8.9 collective-permute-done.1
  453.5 8.9 collective-permute-done.1
  488.8 397.8 %while.46 = (s32[]{:T(128)}, bf16[128,2048]{1,0:T(8,128)(2,1)}, f32[2048,1536]{1,0:T(8,128)}, f32[1024,2048]{1,0:T(8,128)}, s32[]{:T(128)}, /*index=5*/pred[]{:T...) while((s32[]{:T(128)}, bf16[128,2048]{1,0:T(8,128)(2,1)}, ...), condition=%wide.region_25.26_spmd, body=%wide.region_14.25_spmd.sunk | while | flops 3045198336 | bytes 89772920 | solution.py:238
  495.4 30.4 %collective-permute-done.3 = bf16[128,2048]{1,0:T(8,128)(2,1)} collective-permute-done((bf16[128,2048]{1,0:T(8,128)(2,1)S(1)}, bf16[128,2048]{1,0:T(8,128)(2,1)}, u32[]{:S(2)}, u32[]{:S(2)}) %collective-permute-start.3) | collective-permute-done | bytes 524320 | tf_op jit(solution)/shard_map/while/body/eval_jaxpr/ppermute | solution.py:27
  532.7 17.0 %collective-permute-done.3 = bf16[128,2048]{1,0:T(8,128)(2,1)} collective-permute-done((bf16[128,2048]{1,0:T(8,128)(2,1)S(1)}, bf16[128,2048]{1,0:T(8,128)(2,1)}, u32[]{:S(2)}, u32[]{:S(2)}) %collective-permute-start.3) | collective-permute-done | bytes 524320 | tf_op jit(solution)/shard_map/while/body/eval_jaxpr/ppermute | solution.py:27
  556.8 23.9 %collective-permute-done.3 = bf16[128,2048]{1,0:T(8,128)(2,1)} collective-permute-done((bf16[128,2048]{1,0:T(8,128)(2,1)S(1)}, bf16[128,2048]{1,0:T(8,128)(2,1)}, u32[]{:S(2)}, u32[]{:S(2)}) %collective-permute-start.3) | collective-permute-done | bytes 524320 | tf_op jit(solution)/shard_map/while/body/eval_jaxpr/ppermute | solution.py:27
  587.8 17.0 %collective-permute-done.3 = bf16[128,2048]{1,0:T(8,128)(2,1)} collective-permute-done((bf16[128,2048]{1,0:T(8,128)(2,1)S(1)}, bf16[128,2048]{1,0:T(8,128)(2,1)}, u32[]{:S(2)}, u32[]{:S(2)}) %collective-permute-start.3) | collective-permute-done | bytes 524320 | tf_op jit(solution)/shard_map/while/body/eval_jaxpr/ppermute | solution.py:27
  611.9 23.9 %collective-permute-done.3 = bf16[128,2048]{1,0:T(8,128)(2,1)} collective-permute-done((bf16[128,2048]{1,0:T(8,128)(2,1)S(1)}, bf16[128,2048]{1,0:T(8,128)(2,1)}, u32[]{:S(2)}, u32[]{:S(2)}) %collective-permute-start.3) | collective-permute-done | bytes 524320 | tf_op jit(solution)/shard_map/while/body/eval_jaxpr/ppermute | solution.py:27
  642.8 16.3 %collective-permute-done.3 = bf16[128,2048]{1,0:T(8,128)(2,1)} collective-permute-done((bf16[128,2048]{1,0:T(8,128)(2,1)S(1)}, bf16[128,2048]{1,0:T(8,128)(2,1)}, u32[]{:S(2)}, u32[]{:S(2)}) %collective-permute-start.3) | collective-permute-done | bytes 524320 | tf_op jit(solution)/shard_map/while/body/eval_jaxpr/ppermute | solution.py:27
  666.2 172.5 %collective-permute-done.3 = bf16[128,2048]{1,0:T(8,128)(2,1)} collective-permute-done((bf16[128,2048]{1,0:T(8,128)(2,1)S(1)}, bf16[128,2048]{1,0:T(8,128)(2,1)}, u32[]{:S(2)}, u32[]{:S(2)}) %collective-permute-start.3) | collective-permute-done | bytes 524320 | tf_op jit(solution)/shard_map/while/body/eval_jaxpr/ppermute | solution.py:27
  840.0 15.0 %conditional.22 = (bf16[128,1024]{0,1:T(8,128)(2,1)}, bf16[2,128,256]{1,2,0:T(8,128)(2,1)S(1)}, bf16[2,128,256]{1,2,0:T(8,128)(2,1)}) conditional(s32[]{:T(128)} %convert_element_type.320, () %tuple.239, (bf16[128,2048]{1,0:T(8,128)(2,1)S(1)}, bf16[1024,2048]{1,0:T(8,128)(2,1)}, bf16[2,2,128,256]{2,3,1,0:T(8,128)(2,1)}, s32[]{:T(128)}, ...), branch_computations={%region_15.15_spmd, %region_16.18_spmd} | conditional | flops 887359488 | bytes 25409794 | solution.py:210
  858.0 8.2 conditional.23
  867.4 19.1 %conditional.24 = ((f32[2048,1536]{1,0:T(8,128)}, f32[1024,2048]{1,0:T(8,128)})) conditional(s32[]{:T(128)} %convert_element_type.320, (f32[2048,1536]{1,0:T(8,128)}, f32[1024,2048]{1,0:T(8,128)}) %tuple.242, (bf16[2,128,2048]{2,1,0:T(8,128)(2,1)}, s32[]{:T(128)}, bf16[128,1536]{1,0:T(8,128)(2,1)S(1)}, f32[2048,1536]{1,0:T(8,128)}, ...), branch_computations={%region_23.23_spmd, %region_24.24_spmd} | conditional | flops 1347420160 | bytes 43648024 | solution.py:231
  867.5 11.1 convolution_add_fusion.1
  888.0 14.8 %conditional.12 = (bf16[128,1024]{0,1:T(8,128)(2,1)}, bf16[2,128,256]{1,2,0:T(8,128)(2,1)S(1)}, bf16[2,128,256]{1,2,0:T(8,128)(2,1)S(1)}) conditional(s32[]{:T(128)} %convert_element_type.228, () %tuple.147, (bf16[128,2048]{1,0:T(8,128)(2,1)S(1)}, bf16[1024,2048]{1,0:T(8,128)(2,1)}, bf16[2,2,128,256]{2,3,1,0:T(8,128)(2,1)}, s32[]{:T(128)}, ...), branch_computations={%region_26.27_spmd, %region_27.30_spmd} | conditional | flops 887359488 | bytes 25409810 | solution.py:210
  906.2 19.1 %conditional.14 = ((f32[2048,1536]{1,0:T(8,128)}, f32[1024,2048]{1,0:T(8,128)})) conditional(s32[]{:T(128)} %convert_element_type.228, (f32[2048,1536]{1,0:T(8,128)}, f32[1024,2048]{1,0:T(8,128)}) %tuple.145, (bf16[2,128,2048]{2,1,0:T(8,128)(2,1)}, s32[]{:T(128)}, bf16[128,1536]{1,0:T(8,128)(2,1)S(1)}, f32[2048,1536]{1,0:T(8,128)}, ...), branch_computations={%region_32.33_spmd, %region_33.34_spmd} | conditional | flops 1347420160 | bytes 43648024 | solution.py:231
  906.2 11.1 convolution_add_fusion.3
  917.3 8.0 convolution_add_fusion.4
  939.4 86.7 %reduce-scatter.5.cloned.1.call-done = bf16[32,2048]{1,0:T(8,128)(2,1)} async-done(((bf16[1024,2048]{1,0:T(8,128)(2,1)}), bf16[32,2048]{1,0:T(8,128)(2,1)}) %reduce-scatter.5.cloned.1.call-update) | async-done | bytes 131088 | tf_op jit(solution)/shard_map/reduce_scatter | solution.py:244
  1027.7 110.6 %reduce-scatter.3.cloned.1.call-done = bf16[64,1536]{1,0:T(8,128)(2,1)} async-done(((bf16[2048,1536]{1,0:T(8,128)(2,1)}), bf16[64,1536]{1,0:T(8,128)(2,1)}) %reduce-scatter.3.cloned.1.call-update) | async-done | bytes 196624 | tf_op jit(solution)/shard_map/reduce_scatter | solution.py:241
  (434 shorter events, 376.6 us)
Async XLA Ops:
  11.5 172.2 %all-to-all-start = ((bf16[32,64,1536]{2,1,0:T(8,128)(2,1)}), bf16[32,64,1536]{2,1,0:T(8,128)(2,1)}, u32[]{:S(2)}, u32[]{:S(2)}) async-start(bf16[32,64,1536]{2,1,0:T(8,128)(2,1)} %stack.27), calls=%async_computation | async-start | bytes 12582912 | tf_op jit(solution)/shard_map/all_to_all | solution.py:120
  24.3 130.9 %all-gather.3.cloned.1.call-start = ((), (), s32[]{:S(2)}) async-start(), calls=%async_computation.5 | async-start | bytes 4325376 | tf_op jit(solution)/shard_map/all_gather | solution.py:127
  25.0 1001.1 %reduce-scatter.5.cloned.1.call-start = ((), (), s32[]{:S(2)}) async-start(), calls=%async_computation.4 | async-start | bytes 4325376 | tf_op jit(solution)/shard_map/reduce_scatter | solution.py:244
  198.6 6.4 collective-permute-start
  212.8 12.7 %collective-permute-start.1 = (bf16[128,2048]{1,0:T(8,128)(2,1)S(1)}, bf16[128,2048]{1,0:T(8,128)(2,1)S(1)}, u32[]{:S(2)}, u32[]{:S(2)}) collective-permute-start(bf16[128,2048]{1,0:T(8,128)(2,1)S(1)} %get-tuple-element.1417), channel_id=1, source_target_pairs={{0,32},{32,64},{64,96},{96,128},{128,160},{160,192},{192,224},{1,3... | collective-permute-start | bytes 1572872 | tf_op jit(solution)/shard_map/while/body/eval_jaxpr/ppermute | solution.py:27
  235.7 6.7 collective-permute-start
  250.1 15.4 %collective-permute-start.1 = (bf16[128,2048]{1,0:T(8,128)(2,1)S(1)}, bf16[128,2048]{1,0:T(8,128)(2,1)S(1)}, u32[]{:S(2)}, u32[]{:S(2)}) collective-permute-start(bf16[128,2048]{1,0:T(8,128)(2,1)S(1)} %get-tuple-element.1417), channel_id=1, source_target_pairs={{0,32},{32,64},{64,96},{96,128},{128,160},{160,192},{192,224},{1,3... | collective-permute-start | bytes 1572872 | tf_op jit(solution)/shard_map/while/body/eval_jaxpr/ppermute | solution.py:27
  270.4 5.8 collective-permute-start
  277.0 28.7 %collective-permute-start.1 = (bf16[128,2048]{1,0:T(8,128)(2,1)S(1)}, bf16[128,2048]{1,0:T(8,128)(2,1)S(1)}, u32[]{:S(2)}, u32[]{:S(2)}) collective-permute-start(bf16[128,2048]{1,0:T(8,128)(2,1)S(1)} %get-tuple-element.1417), channel_id=1, source_target_pairs={{0,32},{32,64},{64,96},{96,128},{128,160},{160,192},{192,224},{1,3... | collective-permute-start | bytes 1572872 | tf_op jit(solution)/shard_map/while/body/eval_jaxpr/ppermute | solution.py:27
  310.6 5.8 collective-permute-start
  317.2 15.4 %collective-permute-start.1 = (bf16[128,2048]{1,0:T(8,128)(2,1)S(1)}, bf16[128,2048]{1,0:T(8,128)(2,1)S(1)}, u32[]{:S(2)}, u32[]{:S(2)}) collective-permute-start(bf16[128,2048]{1,0:T(8,128)(2,1)S(1)} %get-tuple-element.1417), channel_id=1, source_target_pairs={{0,32},{32,64},{64,96},{96,128},{128,160},{160,192},{192,224},{1,3... | collective-permute-start | bytes 1572872 | tf_op jit(solution)/shard_map/while/body/eval_jaxpr/ppermute | solution.py:27
  337.5 5.8 collective-permute-start
  344.1 26.5 %collective-permute-start.1 = (bf16[128,2048]{1,0:T(8,128)(2,1)S(1)}, bf16[128,2048]{1,0:T(8,128)(2,1)S(1)}, u32[]{:S(2)}, u32[]{:S(2)}) collective-permute-start(bf16[128,2048]{1,0:T(8,128)(2,1)S(1)} %get-tuple-element.1417), channel_id=1, source_target_pairs={{0,32},{32,64},{64,96},{96,128},{128,160},{160,192},{192,224},{1,3... | collective-permute-start | bytes 1572872 | tf_op jit(solution)/shard_map/while/body/eval_jaxpr/ppermute | solution.py:27
  375.5 5.8 collective-permute-start
  382.1 15.4 %collective-permute-start.1 = (bf16[128,2048]{1,0:T(8,128)(2,1)S(1)}, bf16[128,2048]{1,0:T(8,128)(2,1)S(1)}, u32[]{:S(2)}, u32[]{:S(2)}) collective-permute-start(bf16[128,2048]{1,0:T(8,128)(2,1)S(1)} %get-tuple-element.1417), channel_id=1, source_target_pairs={{0,32},{32,64},{64,96},{96,128},{128,160},{160,192},{192,224},{1,3... | collective-permute-start | bytes 1572872 | tf_op jit(solution)/shard_map/while/body/eval_jaxpr/ppermute | solution.py:27
  402.3 5.8 collective-permute-start
  408.9 26.5 %collective-permute-start.1 = (bf16[128,2048]{1,0:T(8,128)(2,1)S(1)}, bf16[128,2048]{1,0:T(8,128)(2,1)S(1)}, u32[]{:S(2)}, u32[]{:S(2)}) collective-permute-start(bf16[128,2048]{1,0:T(8,128)(2,1)S(1)} %get-tuple-element.1417), channel_id=1, source_target_pairs={{0,32},{32,64},{64,96},{96,128},{128,160},{160,192},{192,224},{1,3... | collective-permute-start | bytes 1572872 | tf_op jit(solution)/shard_map/while/body/eval_jaxpr/ppermute | solution.py:27
  440.3 5.8 collective-permute-start
  446.9 15.4 %collective-permute-start.1 = (bf16[128,2048]{1,0:T(8,128)(2,1)S(1)}, bf16[128,2048]{1,0:T(8,128)(2,1)S(1)}, u32[]{:S(2)}, u32[]{:S(2)}) collective-permute-start(bf16[128,2048]{1,0:T(8,128)(2,1)S(1)} %get-tuple-element.1417), channel_id=1, source_target_pairs={{0,32},{32,64},{64,96},{96,128},{128,160},{160,192},{192,224},{1,3... | collective-permute-start | bytes 1572872 | tf_op jit(solution)/shard_map/while/body/eval_jaxpr/ppermute | solution.py:27
  467.2 8.7 collective-permute-start.4
  494.1 31.7 %collective-permute-start.3 = (bf16[128,2048]{1,0:T(8,128)(2,1)S(1)}, bf16[128,2048]{1,0:T(8,128)(2,1)}, u32[]{:S(2)}, u32[]{:S(2)}) collective-permute-start(bf16[128,2048]{1,0:T(8,128)(2,1)S(1)} %get-tuple-element.1444), channel_id=1, source_target_pairs={{32,0},{64,32},{96,64},{128,96},{160,128},{192,160},{224,192},{33,... | collective-permute-start | bytes 1572872 | tf_op jit(solution)/shard_map/while/body/eval_jaxpr/ppermute | solution.py:27
  531.4 18.3 %collective-permute-start.3 = (bf16[128,2048]{1,0:T(8,128)(2,1)S(1)}, bf16[128,2048]{1,0:T(8,128)(2,1)}, u32[]{:S(2)}, u32[]{:S(2)}) collective-permute-start(bf16[128,2048]{1,0:T(8,128)(2,1)S(1)} %get-tuple-element.1444), channel_id=1, source_target_pairs={{32,0},{64,32},{96,64},{128,96},{160,128},{192,160},{224,192},{33,... | collective-permute-start | bytes 1572872 | tf_op jit(solution)/shard_map/while/body/eval_jaxpr/ppermute | solution.py:27
  555.5 25.2 %collective-permute-start.3 = (bf16[128,2048]{1,0:T(8,128)(2,1)S(1)}, bf16[128,2048]{1,0:T(8,128)(2,1)}, u32[]{:S(2)}, u32[]{:S(2)}) collective-permute-start(bf16[128,2048]{1,0:T(8,128)(2,1)S(1)} %get-tuple-element.1444), channel_id=1, source_target_pairs={{32,0},{64,32},{96,64},{128,96},{160,128},{192,160},{224,192},{33,... | collective-permute-start | bytes 1572872 | tf_op jit(solution)/shard_map/while/body/eval_jaxpr/ppermute | solution.py:27
  584.4 1.9 collective-permute-start.2
  586.4 18.3 %collective-permute-start.3 = (bf16[128,2048]{1,0:T(8,128)(2,1)S(1)}, bf16[128,2048]{1,0:T(8,128)(2,1)}, u32[]{:S(2)}, u32[]{:S(2)}) collective-permute-start(bf16[128,2048]{1,0:T(8,128)(2,1)S(1)} %get-tuple-element.1444), channel_id=1, source_target_pairs={{32,0},{64,32},{96,64},{128,96},{160,128},{192,160},{224,192},{33,... | collective-permute-start | bytes 1572872 | tf_op jit(solution)/shard_map/while/body/eval_jaxpr/ppermute | solution.py:27
  610.5 25.2 %collective-permute-start.3 = (bf16[128,2048]{1,0:T(8,128)(2,1)S(1)}, bf16[128,2048]{1,0:T(8,128)(2,1)}, u32[]{:S(2)}, u32[]{:S(2)}) collective-permute-start(bf16[128,2048]{1,0:T(8,128)(2,1)S(1)} %get-tuple-element.1444), channel_id=1, source_target_pairs={{32,0},{64,32},{96,64},{128,96},{160,128},{192,160},{224,192},{33,... | collective-permute-start | bytes 1572872 | tf_op jit(solution)/shard_map/while/body/eval_jaxpr/ppermute | solution.py:27
  639.5 1.9 collective-permute-start.2
  641.5 17.6 %collective-permute-start.3 = (bf16[128,2048]{1,0:T(8,128)(2,1)S(1)}, bf16[128,2048]{1,0:T(8,128)(2,1)}, u32[]{:S(2)}, u32[]{:S(2)}) collective-permute-start(bf16[128,2048]{1,0:T(8,128)(2,1)S(1)} %get-tuple-element.1444), channel_id=1, source_target_pairs={{32,0},{64,32},{96,64},{128,96},{160,128},{192,160},{224,192},{33,... | collective-permute-start | bytes 1572872 | tf_op jit(solution)/shard_map/while/body/eval_jaxpr/ppermute | solution.py:27
  664.8 173.9 %collective-permute-start.3 = (bf16[128,2048]{1,0:T(8,128)(2,1)S(1)}, bf16[128,2048]{1,0:T(8,128)(2,1)}, u32[]{:S(2)}, u32[]{:S(2)}) collective-permute-start(bf16[128,2048]{1,0:T(8,128)(2,1)S(1)} %get-tuple-element.1444), channel_id=1, source_target_pairs={{32,0},{64,32},{96,64},{128,96},{160,128},{192,160},{224,192},{33,... | collective-permute-start | bytes 1572872 | tf_op jit(solution)/shard_map/while/body/eval_jaxpr/ppermute | solution.py:27
  866.1 20.6 %collective-permute-start.3 = (bf16[128,2048]{1,0:T(8,128)(2,1)S(1)}, bf16[128,2048]{1,0:T(8,128)(2,1)}, u32[]{:S(2)}, u32[]{:S(2)}) collective-permute-start(bf16[128,2048]{1,0:T(8,128)(2,1)S(1)} %get-tuple-element.1444), channel_id=1, source_target_pairs={{32,0},{64,32},{96,64},{128,96},{160,128},{192,160},{224,192},{33,... | collective-permute-start | bytes 1572872 | tf_op jit(solution)/shard_map/while/body/eval_jaxpr/ppermute | solution.py:27
  902.9 1.9 collective-permute-start.5
  931.4 206.9 %reduce-scatter.3.cloned.1.call-start = ((), (), s32[]{:S(2)}) async-start(), calls=%async_computation.3 | async-start | bytes 6488064 | tf_op jit(solution)/shard_map/reduce_scatter | solution.py:241
  (23 other events, 65.2 us)
Sparse Core Ops, SparseCore 0:
  27.6 127.4 all-gather.2
  931.5 94.5 reduce-scatter.4
  1030.6 107.5 reduce-scatter.2
